TPU v7x, 512 devices: a whole 4x8x8 slice. The times are simulated.
512 devices in a mesh: dp: 128 (over y, z, core), shard: 4 (over x).
Axes of the slice: x: 4, y: 8, z: 8, core: 2. Of those that a mesh axis runs over, the one named last changes fastest.
Arguments:
- acts: bfloat16 [131072, 1792], P('dp', 'shard'), may hold values from -6 to 6
- grad_out: bfloat16 [131072, 3584], P('dp', 'shard'), may hold values from -0.016479492 to 0.016479492
- projector: bfloat16 [1792, 256], P('shard'), may hold values from -6 to 6
- moment: bfloat16 [256, 3584], P(None, 'shard'), may hold values from -4 to 4
- second: bfloat16 [256, 3584], P(None, 'shard'), may hold values from 0.29882812 to 3
Outputs:
- new_projector: bfloat16 [1792, 256], P('shard')
- new_moment: bfloat16 [256, 3584], P(None, 'shard')
- new_second: bfloat16 [256, 3584], P(None, 'shard')
- weight_update: bfloat16 [1792, 3584], P('dp', 'shard')
All inputs are finite; a program needn't handle non-finite values.
Results may differ from a plain program's by a relative error of at most 0.0055.
Values may be sent and summed in bfloat16 or wider, within the bound.
A program may use at most 64 MiB of HBM per device.

v0:
```python
import jax
import jax.numpy as jnp
from jax import lax
from jax.sharding import PartitionSpec as P

D = 1792
RANK = 256


def shards(acts, grad_out, projector, moment, second):
    inv_width = 1.0 / D**0.5
    partial_value = jnp.dot(acts, projector, preferred_element_type=jnp.float32)
    summed = lax.psum(partial_value, "shard")
    proj_acts = (summed * inv_width).astype(jnp.bfloat16)
    local_grad = jnp.einsum("tr,tf->rf", proj_acts, grad_out, preferred_element_type=jnp.float32)
    proj_grad = lax.psum(local_grad, "dp")
    proj_low = proj_grad.astype(jnp.bfloat16)
    score_terms = jnp.einsum("tf,rf->tr", grad_out, proj_low, preferred_element_type=jnp.float32)
    token_scores = lax.psum(score_terms, "shard").astype(jnp.bfloat16)
    local_sub = jnp.einsum("td,tr->dr", acts, token_scores, preferred_element_type=jnp.float32)
    subspace = lax.psum(local_sub, "dp")
    gram_local = jnp.dot(
        subspace.T, subspace, precision=lax.Precision.HIGHEST, preferred_element_type=jnp.float32
    )
    gram_matrix = lax.psum(gram_local, "shard")
    mean_square = jnp.trace(gram_matrix) / (D * RANK) + 1e-06
    cubic = jnp.dot(
        subspace, gram_matrix, precision=lax.Precision.HIGHEST, preferred_element_type=jnp.float32
    )
    new_projector = (
        (1.5 * subspace - 0.5 * cubic / (mean_square * D)) / jnp.sqrt(mean_square)
    ).astype(jnp.bfloat16)
    moment_f = 0.9 * moment.astype(jnp.float32) + 0.1 * proj_grad
    second_f = 0.95 * second.astype(jnp.float32) + 0.05 * proj_grad * proj_grad
    first_fix = 1.0 - 0.9**20
    second_fix = 1.0 - 0.95**20
    direction = (moment_f / first_fix / (jnp.sqrt(second_f / second_fix) + 1e-08)).astype(
        jnp.bfloat16
    )
    row_count = D // lax.axis_size("dp")
    replica = lax.axis_index("dp")
    all_rows = lax.all_gather(projector, "shard", axis=0, tiled=True)
    own_rows = lax.dynamic_slice_in_dim(all_rows, replica * row_count, row_count, 0)
    weight_update = (
        jnp.dot(own_rows, direction, preferred_element_type=jnp.float32) / RANK**0.5
    ).astype(jnp.bfloat16)
    return (
        new_projector,
        moment_f.astype(jnp.bfloat16),
        second_f.astype(jnp.bfloat16),
        weight_update,
    )


def solution(mesh):
    in_specs = (
        P("dp", "shard"),
        P("dp", "shard"),
        P("shard", None),
        P(None, "shard"),
        P(None, "shard"),
    )
    out_specs = (P("shard", None), P(None, "shard"), P(None, "shard"), P("dp", "shard"))
    return jax.shard_map(shards, mesh=mesh, in_specs=in_specs, out_specs=out_specs, check_vma=False)
```

profile of v0, /device:TPU:8, one launch (start us, length us, event | category | flops | bytes accessed | tf_op | source)
XLA Modules:
  0.0 563.3 jit_solution(5339090869765811914)
XLA Ops:
  7.2 0.0 copy-start
  7.2 0.0 all-reduce.6.cloned.1.call-start
  7.2 2.9 fusion.22
  10.1 0.0 all-reduce.6.cloned.1.call-update
  10.1 0.0 copy-start.3
  10.1 0.0 all-reduce.8.cloned.1.call-start
  10.2 61.5 %all-reduce.6.cloned.1.call-done = f32[1024,256]{1,0:T(8,128)} async-done(((f32[1024,256]{1,0:T(8,128)}), f32[1024,256]{1,0:T(8,128)}) %all-reduce.6.cloned.1.call-update) | async-done | bytes 1048592 | tf_op jit(solution)/shard_map/psum | solution.py:13
  71.7 0.0 copy-done
  71.7 2.9 fusion.7
  74.6 0.0 all-reduce.8.cloned.1.call-update
  74.7 0.0 all-reduce.10.cloned.1.call-start
  74.7 0.0 copy-done.3
  74.7 15.0 %all_gather.3 = bf16[1792,256]{1,0:T(8,128)(2,1)} all-gather(bf16[448,256]{1,0:T(8,128)(2,1)S(1)} %copy-done.3), channel_id=1, replica_groups=mesh['dp'=128,'shard'=4] {'shard'}, dimensions={0}, use_global_device_ids=true | all-gather | bytes 1146880 | tf_op jit(solution)/shard_map/all_gather | solution.py:42
  89.8 183.2 %all-reduce.8.cloned.1.call-done = f32[256,896]{1,0:T(8,128)} async-done(((f32[256,896]{1,0:T(8,128)}), f32[256,896]{1,0:T(8,128)}) %all-reduce.8.cloned.1.call-update) | async-done | bytes 917520 | tf_op jit(solution)/shard_map/psum | solution.py:16
  273.0 1.9 convolution_bitcast_fusion
  274.9 33.3 %all-reduce.13 = bf16[1024,256]{0,1:T(8,128)(2,1)S(1)} all-reduce(f32[1024,256]{0,1:T(8,128)S(1)} %convolution_bitcast_fusion), channel_id=1, replica_groups=mesh['dp'=128,'shard'=4] {'shard'}, use_global_device_ids=true, to_apply=%region_2.0 | all-reduce | flops 262144 | bytes 1572864 | tf_op jit(solution)/shard_map/psum | solution.py:19
  308.2 0.0 copy-start.1
  308.2 2.5 convolution_bitcast_fusion.1
  310.7 0.0 all-reduce.10.cloned.1.call-update
  310.7 0.0 all-reduce.12.cloned.1.call-start
  310.8 0.0 copy-done.1
  310.8 2.6 fusion.4
  313.4 186.1 %all-reduce.10.cloned.1.call-done = f32[448,256]{1,0:T(8,128)} async-done(((f32[448,256]{1,0:T(8,128)}), f32[448,256]{1,0:T(8,128)}) %all-reduce.10.cloned.1.call-update) | async-done | bytes 458768 | tf_op jit(solution)/shard_map/psum | solution.py:21
  499.4 2.9 fusion.23
  502.3 0.0 copy-start.2
  502.3 0.0 all-reduce.12.cloned.1.call-update
  502.3 2.4 fusion.10
  504.8 47.5 %all-reduce.12.cloned.1.call-done = f32[256,256]{1,0:T(8,128)} async-done(((f32[256,256]{1,0:T(8,128)}), f32[256,256]{1,0:T(8,128)}) %all-reduce.12.cloned.1.call-update) | async-done | bytes 262160 | tf_op jit(solution)/shard_map/psum | solution.py:25
  552.2 1.6 select_reduce_fusion
  554.5 0.0 copy-done.2
  554.5 2.2 fusion.3
Async XLA Ops:
  7.2 64.6 %copy-start = (bf16[1024,896]{1,0:T(8,128)(2,1)S(1)}, bf16[1024,896]{1,0:T(8,128)(2,1)}, u32[]{:S(2)}) copy-start(bf16[1024,896]{1,0:T(8,128)(2,1)} %param.6) | copy-start | bytes 5505028
  7.2 64.5 %all-reduce.6.cloned.1.call-start = ((), (), s32[]{:S(2)}) async-start(), calls=%async_computation | async-start | bytes 2097152 | tf_op jit(solution)/shard_map/psum | solution.py:13
  10.1 64.6 %copy-start.3 = (bf16[448,256]{1,0:T(8,128)(2,1)S(1)}, bf16[448,256]{1,0:T(8,128)(2,1)}, u32[]{:S(2)}) copy-start(bf16[448,256]{1,0:T(8,128)(2,1)} %param.7) | copy-start | bytes 688132
  10.1 262.9 %all-reduce.8.cloned.1.call-start = ((), (), s32[]{:S(2)}) async-start(), calls=%async_computation.1 | async-start | bytes 1835008 | tf_op jit(solution)/shard_map/psum | solution.py:16
  74.7 424.8 %all-reduce.10.cloned.1.call-start = ((), (), s32[]{:S(2)}) async-start(), calls=%async_computation.2 | async-start | bytes 917504 | tf_op jit(solution)/shard_map/psum | solution.py:21
  308.2 2.6 copy-start.1
  310.7 241.5 %all-reduce.12.cloned.1.call-start = ((), (), s32[]{:S(2)}) async-start(), calls=%async_computation.3 | async-start | bytes 524288 | tf_op jit(solution)/shard_map/psum | solution.py:25
  502.3 52.2 %copy-start.2 = (f32[448,256]{1,0:T(8,128)S(1)}, f32[448,256]{1,0:T(8,128)}, u32[]{:S(2)}) copy-start(f32[448,256]{1,0:T(8,128)} %all-reduce.10.cloned.1.call-done) | copy-start | bytes 1376260
Sparse Core Ops, SparseCore 0:
  10.3 61.3 all-reduce.5
  75.0 197.9 all-reduce.7
  310.9 188.5 all-reduce.9
  502.5 49.7 all-reduce.11
where the time goes:
time: 564 us; the launch traced here: 563 us
  waiting for transfers between devices  478 us (85%)
  blocking collectives  48.4 us (9%)
  matrix products  17.8 us (3%)
  between operations  14.5 us (3%)
    psum x1, waiting for transfers between devices, shards(): subspace = lax.psum(local_sub, 'dp')  186 us
    psum x1, waiting for transfers between devices, shards(): proj_grad = lax.psum(local_grad, 'dp')  183 us
    psum x1, waiting for transfers between devices, shards(): summed = lax.psum(partial_value, 'shard')  61.5 us
    psum x1, waiting for transfers between devices, shards(): gram_matrix = lax.psum(gram_local, 'shard')  47.5 us
    psum x1, blocking collectives, shards(): token_scores = lax.psum(score_terms, 'shard').astype(jnp.bfloat16)  33.3 us
    all_gather x1, blocking collectives, shards(): all_rows = lax.all_gather(projector, 'shard', axis=0, tiled=True)  15 us
  transfers between devices with their start and end apart: 4, of which 4 were waited for; matrix products, arithmetic and copies ran while one was open for 1% of the time, Pallas kernels for 0%

commit v1 on v0

--- a/solution.py
+++ b/solution.py
@@ -18,7 +18,8 @@
     score_terms = jnp.einsum("tf,rf->tr", grad_out, proj_low, preferred_element_type=jnp.float32)
     token_scores = lax.psum(score_terms, "shard").astype(jnp.bfloat16)
     local_sub = jnp.einsum("td,tr->dr", acts, token_scores, preferred_element_type=jnp.float32)
-    subspace = lax.psum(local_sub, "dp")
+    blocks = lax.all_gather(local_sub, "dp")
+    subspace = jnp.sum(blocks, axis=0)
     gram_local = jnp.dot(
         subspace.T, subspace, precision=lax.Precision.HIGHEST, preferred_element_type=jnp.float32
     )

time: 564 us -> 592 us (1.050)
  other arithmetic: 4.02 us -> 21.4 us
  waiting for transfers between devices: 478 us -> 493 us
    psum x1 -> x0, waiting for transfers between devices: 186 us -> none  [shards(): subspace = lax.psum(local_sub, 'dp')]
    all_gather x0 -> x1, waiting for transfers between devices: none -> 184 us  [shards(): blocks = lax.all_gather(local_sub, 'dp')]
    reduce_sum x0 -> x1, other arithmetic: none -> 18.5 us  [shards(): subspace = jnp.sum(blocks, axis=0)]
    psum x1, waiting for transfers between devices: 183 us -> 198 us  [shards(): proj_grad = lax.psum(local_grad, 'dp')]
  transfers between devices with their start and end apart: 4 -> 4, of which waited for: 4 -> 4; matrix products, arithmetic and copies ran while one was open for 1% -> 0% of each run, Pallas kernels for 0% -> 0%
where the time goes in v1:
time: 592 us
  waiting for transfers between devices  493 us (83%)
  blocking collectives  47 us (8%)
  other arithmetic  21.4 us (4%)
  matrix products  15.5 us (3%)
  between operations  14.5 us (2%)
    psum x1, waiting for transfers between devices, shards(): proj_grad = lax.psum(local_grad, 'dp')  198 us
    all_gather x1, waiting for transfers between devices, shards(): blocks = lax.all_gather(local_sub, 'dp')  184 us
    psum x1, waiting for transfers between devices, shards(): summed = lax.psum(partial_value, 'shard')  61.6 us
    psum x1, waiting for transfers between devices, shards(): gram_matrix = lax.psum(gram_local, 'shard')  49.4 us
    psum x1, blocking collectives, shards(): token_scores = lax.psum(score_terms, 'shard').astype(jnp.bfloat16)  33.4 us
    reduce_sum x1, other arithmetic, shards(): subspace = jnp.sum(blocks, axis=0)  18.5 us
    all_gather x1, blocking collectives, shards(): all_rows = lax.all_gather(projector, 'shard', axis=0, tiled=True)  13.6 us
  transfers between devices with their start and end apart: 4, of which 4 were waited for; matrix products, arithmetic and copies ran while one was open for 0% of the time, Pallas kernels for 0%

profile of v1, /device:TPU:8, one launch (start us, length us, event | category | flops | bytes accessed | tf_op | source)
XLA Modules:
  0.0 591.7 jit_solution(18061671478976616150)
XLA Ops:
  7.2 0.0 copy-start
  7.2 0.0 all-reduce.5.cloned.1.call-start
  7.2 2.9 fusion.22
  10.1 0.0 all-reduce.5.cloned.1.call-update
  10.1 0.0 all-reduce.7.cloned.1.call-start
  10.2 61.6 %all-reduce.5.cloned.1.call-done = f32[1024,256]{1,0:T(8,128)} async-done(((f32[1024,256]{1,0:T(8,128)}), f32[1024,256]{1,0:T(8,128)}) %all-reduce.5.cloned.1.call-update) | async-done | bytes 1048592 | tf_op jit(solution)/shard_map/psum | solution.py:13
  71.7 0.0 copy-done
  71.7 2.9 fusion.7
  74.7 0.0 all-reduce.7.cloned.1.call-update
  74.7 0.0 all-gather.3.cloned.1.call-start
  74.7 198.3 %all-reduce.7.cloned.1.call-done = f32[256,896]{1,0:T(8,128)} async-done(((f32[256,896]{1,0:T(8,128)}), f32[256,896]{1,0:T(8,128)}) %all-reduce.7.cloned.1.call-update) | async-done | bytes 917520 | tf_op jit(solution)/shard_map/psum | solution.py:16
  273.0 1.9 convolution_bitcast_fusion
  274.9 0.0 copy-start.3
  275.0 33.4 %all-reduce.10 = bf16[1024,256]{0,1:T(8,128)(2,1)S(1)} all-reduce(f32[1024,256]{0,1:T(8,128)S(1)} %convolution_bitcast_fusion), channel_id=1, replica_groups=mesh['dp'=128,'shard'=4] {'shard'}, use_global_device_ids=true, to_apply=%region_2.0 | all-reduce | flops 262144 | bytes 1572864 | tf_op jit(solution)/shard_map/psum | solution.py:19
  308.4 0.0 copy-start.2
  308.4 0.0 copy-start.4
  308.4 0.0 copy-start.5
  308.4 2.5 convolution_bitcast_fusion.1
  311.0 0.0 all-gather.3.cloned.1.call-update
  311.0 0.0 all-reduce.9.cloned.1.call-start
  311.0 0.0 copy-done.3
  311.1 13.6 %all_gather.11 = bf16[1792,256]{1,0:T(8,128)(2,1)S(1)} all-gather(bf16[448,256]{1,0:T(8,128)(2,1)S(1)} %copy-done.3), channel_id=1, replica_groups=mesh['dp'=128,'shard'=4] {'shard'}, dimensions={0}, use_global_device_ids=true | all-gather | bytes 1146880 | tf_op jit(solution)/shard_map/all_gather | solution.py:43
  324.6 0.0 copy-done.4
  324.6 1.4 fusion.4
  326.0 183.8 %all-gather.3.cloned.1.call-done = f32[57344,256]{1,0:T(8,128)} async-done(((f32[448,256]{1,0:T(8,128)}), f32[57344,256]{1,0:T(8,128)}) %all-gather.3.cloned.1.call-update) | async-done | bytes 58720272 | tf_op jit(solution)/shard_map/all_gather | solution.py:21
  509.8 18.5 %reduce_sum.19 = f32[448,256]{1,0:T(8,128)S(1)} reduce(f32[128,448,256]{2,1,0:T(8,128)} %bitcast.15, f32[]{:T(128)} %constant.21.clone.1), dimensions={0}, to_apply=%region_3.0 | reduce | flops 14565376 | bytes 59179012 | tf_op jit(solution)/shard_map/reduce_sum | solution.py:22
  528.2 1.7 fusion.23
  530.0 0.0 all-reduce.9.cloned.1.call-update
  530.0 1.2 fusion.10
  531.2 49.4 %all-reduce.9.cloned.1.call-done = f32[256,256]{1,0:T(8,128)} async-done(((f32[256,256]{1,0:T(8,128)}), f32[256,256]{1,0:T(8,128)}) %all-reduce.9.cloned.1.call-update) | async-done | bytes 262160 | tf_op jit(solution)/shard_map/psum | solution.py:26
  580.6 1.7 select_reduce_fusion
  583.0 2.2 fusion.3
  (4 shorter events, 0.0 us)
Async XLA Ops:
  7.2 64.6 %copy-start = (bf16[1024,896]{1,0:T(8,128)(2,1)S(1)}, bf16[1024,896]{1,0:T(8,128)(2,1)}, u32[]{:S(2)}) copy-start(bf16[1024,896]{1,0:T(8,128)(2,1)} %param.6) | copy-start | bytes 5505028
  7.2 64.5 %all-reduce.5.cloned.1.call-start = ((), (), s32[]{:S(2)}) async-start(), calls=%async_computation | async-start | bytes 2097152 | tf_op jit(solution)/shard_map/psum | solution.py:13
  10.1 262.9 %all-reduce.7.cloned.1.call-start = ((), (), s32[]{:S(2)}) async-start(), calls=%async_computation.1 | async-start | bytes 1835008 | tf_op jit(solution)/shard_map/psum | solution.py:16
  74.7 435.1 %all-gather.3.cloned.1.call-start = ((), (), s32[]{:S(2)}) async-start(), calls=%async_computation.3 | async-start | bytes 59179008 | tf_op jit(solution)/shard_map/all_gather | solution.py:21
  274.9 36.1 %copy-start.3 = (bf16[448,256]{1,0:T(8,128)(2,1)S(1)}, bf16[448,256]{1,0:T(8,128)(2,1)}, u32[]{:S(2)}) copy-start(bf16[448,256]{1,0:T(8,128)(2,1)} %param.7) | copy-start | bytes 688132
  308.4 16.2 %copy-start.2 = (f32[256,896]{1,0:T(8,128)S(1)}, f32[256,896]{1,0:T(8,128)}, u32[]{:S(2)}) copy-start(f32[256,896]{1,0:T(8,128)} %all-reduce.7.cloned.1.call-done) | copy-start | bytes 2752516
  308.4 16.2 %copy-start.4 = (bf16[256,896]{1,0:T(8,128)(2,1)S(1)}, bf16[256,896]{1,0:T(8,128)(2,1)}, u32[]{:S(2)}) copy-start(bf16[256,896]{1,0:T(8,128)(2,1)} %param.9) | copy-start | bytes 1376260
  308.4 16.2 %copy-start.5 = (bf16[256,896]{1,0:T(8,128)(2,1)S(1)}, bf16[256,896]{1,0:T(8,128)(2,1)}, u32[]{:S(2)}) copy-start(bf16[256,896]{1,0:T(8,128)(2,1)} %param.8) | copy-start | bytes 1376260
  311.0 269.6 %all-reduce.9.cloned.1.call-start = ((), (), s32[]{:S(2)}) async-start(), calls=%async_computation.2 | async-start | bytes 524288 | tf_op jit(solution)/shard_map/psum | solution.py:26
  580.6 4.6 copy-start.1
Sparse Core Ops, SparseCore 0:
  10.3 61.3 all-reduce.4
  75.0 197.9 all-reduce.6
  311.1 198.6 all-gather.2
  530.1 50.4 all-reduce.8
